TPU v7x, 32 devices: a whole 2x2x4 slice. The times are simulated.
32 devices in a mesh: chaos: 8 (over z, x), space: 4 (over y, core).
Axes of the slice: x: 2, y: 2, z: 4, core: 2. Of those that a mesh axis runs over, the one named last changes fastest.
Arguments:
- coeffs: float32 [64, 16, 32, 128], P('chaos', 'space'), may hold values from -6 to 6
- source: float32 [64, 16, 32, 128], P('chaos', 'space'), may hold values from -6 to 6
- mean_field: float32 [16, 32, 128], P('space'), may hold values from 0.5 to 2
- mode_bank: float32 [8, 16, 32, 128], P('chaos', 'space'), may hold values from -2.4 to 2.4
- mode_owner: int32 [2], replicated, may hold values from 0 to 7, as said below
- links: int32 [8, 32, 4], P('chaos'), may hold values from 0 to 63, as said below
Outputs:
- residual: float32 [64, 16, 32, 128], P('chaos', 'space')
- correction: float32 [64, 16, 32, 128], P('chaos', 'space')
Inputs may be any that keep to these rules, and one draw needn't show every extreme that they name: `mode_owner`: 2 distinct slots. Entry (s, p, k, L) of links[d]: s a coefficient among device d's 8, p a global destination coefficient, k a mode, L a level from 0 to 3, where level 0 marks a pair that is absent. Every pair appears in both directions with one level. One device's list names coefficients of one destination device at most 5 times, and some device's list does so exactly 5 times with all those entries present.
All inputs are finite; a program needn't handle non-finite values.
Results may differ from a plain program's by a relative error of at most 0.00015.
Values sent between devices are 32-bit elements; how exact they have to be, the bound alone decides.
No kernel may reach another device: no remote copies, remote signals or barrier semaphores. Data moves between devices by JAX's collectives and lax.ppermute only.
A program may use at most 128 MiB of HBM per device.

v0:
```python
import jax
import jax.numpy as jnp
from jax import lax
from jax.sharding import PartitionSpec as P

M = 2
ITERS = 4
REACTION = 0.5
BOUND_LOW = 0.04
BOUND_HIGH = 2.0


def spread(array, axis, root):
    mine = lax.axis_index(axis) == root
    return lax.psum(jnp.where(mine, array, jnp.zeros_like(array)), axis)


def extended_2(cells, sides, width):
    for axis, dim in sides:
        count = lax.axis_size(axis)
        ends = count - 1
        head = lax.slice_in_dim(cells, 0, width, axis=dim)
        tail = lax.slice_in_dim(cells, cells.shape[dim] - width, cells.shape[dim], axis=dim)
        cells = jnp.concatenate(
            [
                lax.ppermute(tail, axis, [(i, (i + 1) % count) for i in range(ends)]),
                cells,
                lax.ppermute(head, axis, [((i + 1) % count, i) for i in range(ends)]),
            ],
            axis=dim,
        )
    return cells


def neighbour(values, along_axis, offset):
    along_axis = along_axis % values.ndim
    length = values.shape[along_axis]
    zero_rim = jnp.zeros_like(lax.slice_in_dim(values, 0, 1, axis=along_axis))
    if offset > 0:
        return jnp.concatenate(
            [lax.slice_in_dim(values, 1, length, axis=along_axis), zero_rim], axis=along_axis
        )
    return jnp.concatenate(
        [zero_rim, lax.slice_in_dim(values, 0, length - 1, axis=along_axis)], axis=along_axis
    )


def neighbour_pairs(values, diffusion):
    centre = values[..., 1:-1, :, :]
    own_coef = diffusion[..., 1:-1, :, :]
    listing = [
        (values[..., 2:, :, :], diffusion[..., 2:, :, :]),
        (values[..., :-2, :, :], diffusion[..., :-2, :, :]),
    ]
    for along_axis in (-2, -1):
        for offset in (1, -1):
            listing.append(
                (neighbour(centre, along_axis, offset), neighbour(own_coef, along_axis, offset))
            )
    return (centre, own_coef, listing)


def stencil(values, diffusion):
    centre, own_coef, listing = neighbour_pairs(values, diffusion)
    running = None
    for other_cell, near_coef in listing:
        term = 0.5 * (own_coef + near_coef) * (centre - other_cell)
        running = term if running is None else running + term
    return running


def face_total(diffusion):
    centre, own_coef, listing = neighbour_pairs(diffusion, diffusion)
    running = None
    for other_cell, near_coef in listing:
        term = 0.5 * (own_coef + near_coef)
        running = term if running is None else running + term
    return running


def per_device(coeffs, source, mean_field, mode_bank, mode_owner, links):
    coef_dev = coeffs.shape[0]
    cell_count = coeffs.shape[1] * coeffs.shape[2] * coeffs.shape[3]
    chaos_count = lax.axis_size("chaos")
    bank_slot = mode_bank[0]
    fields = [spread(bank_slot, "chaos", mode_owner[number]) for number in range(M)]
    mode_fields = jnp.stack(fields)
    stacked = jnp.concatenate([coeffs, mean_field[None], mode_fields], axis=0)
    extended = extended_2(stacked, (("space", 1),), 1)
    coef_ext = extended[:coef_dev]
    mean_ext = extended[coef_dev]
    mode_ext = extended[coef_dev + 1 :]
    base_apply = REACTION * coeffs + stencil(coef_ext, mean_ext)
    entries = links[0]
    src_local = entries[:, 0]
    dst_global = entries[:, 1]
    mode_ids = entries[:, 2]
    levels = entries[:, 3]
    weight = jnp.sqrt(levels.astype(jnp.float32))
    dest_dev = dst_global // coef_dev
    dst_local = dst_global % coef_dev
    raise_count = M * coef_dev
    shift_range = chaos_count // 2 - 1
    capacity = max(2, (raise_count - 1 + shift_range - 1) // shift_range)
    onehot_dest = (dest_dev[:, None] == jnp.arange(chaos_count)[None, :]).astype(jnp.int32)
    bucket_rank = jnp.sum(jnp.cumsum(onehot_dest, axis=0) * onehot_dest, axis=1) - 1
    slot_index = dest_dev * capacity + bucket_rank
    slot_table = (jnp.arange(chaos_count * capacity)[:, None] == slot_index[None, :]).astype(
        jnp.int32
    )
    payload = coeffs.reshape(coef_dev, cell_count)
    target_tag = dst_local * M + mode_ids
    target_count = coef_dev * M
    row_table = (src_local[:, None] == jnp.arange(payload.shape[0])[None, :]).astype(
        jnp.float32
    ) * weight[:, None]
    send_matrix = jnp.dot(
        slot_table.astype(jnp.float32), row_table, precision=lax.Precision.HIGHEST
    )
    send_block = jnp.dot(send_matrix, payload, precision=lax.Precision.HIGHEST)
    send_block = send_block.reshape(chaos_count, capacity, cell_count)
    live_tag = jnp.where(levels > 0, target_tag, -1)
    slot_ids = jnp.sum(slot_table * (live_tag + 1)[None, :], axis=1) - 1
    slot_ids = slot_ids.reshape(chaos_count, capacity)
    received, received_ids = (
        lax.all_to_all(send_block, "chaos", split_axis=0, concat_axis=0, tiled=True),
        lax.all_to_all(slot_ids, "chaos", split_axis=0, concat_axis=0, tiled=True),
    )
    received_flat = received.reshape(chaos_count * capacity, cell_count)
    gather_table = (jnp.arange(target_count)[:, None] == received_ids.reshape(-1)[None, :]).astype(
        jnp.float32
    )
    summed = jnp.dot(gather_table, received_flat, precision=lax.Precision.HIGHEST)
    combined = summed.reshape(coef_dev, M, coeffs.shape[1], coeffs.shape[2], coeffs.shape[3])
    combined_ext = extended_2(combined, (("space", 2),), 1)
    coupling = None
    for mode_index in range(M):
        term = stencil(combined_ext[:, mode_index], mode_ext[mode_index])
        coupling = term if coupling is None else coupling + term
    residual = source - (base_apply + coupling)
    diagonal = REACTION + face_total(mean_ext)
    midpoint = (BOUND_HIGH + BOUND_LOW) / 2.0
    halfwidth = (BOUND_HIGH - BOUND_LOW) / 2.0
    spread_ratio = midpoint / halfwidth
    update = residual / (midpoint * diagonal)
    ratio_now = 1.0 / spread_ratio
    solution = jnp.zeros_like(residual)
    remainder = residual
    for sweep_index in range(ITERS):
        solution = solution + update
        if sweep_index + 1 < ITERS:
            update_ext = extended_2(update, (("space", 1),), 1)
            remainder = remainder - (REACTION * update + stencil(update_ext, mean_ext))
            ratio_next = 1.0 / (2.0 * spread_ratio - ratio_now)
            update = (
                ratio_next * ratio_now * update
                + 2.0 * ratio_next / halfwidth * remainder / diagonal
            )
            ratio_now = ratio_next
    return (residual, solution)


def solution(mesh):
    in_specs = (
        P("chaos", "space", None, None),
        P("chaos", "space", None, None),
        P("space", None, None),
        P("chaos", "space", None, None),
        P(),
        P("chaos", None, None),
    )
    out_specs = (P("chaos", "space", None, None), P("chaos", "space", None, None))
    return jax.shard_map(
        per_device, mesh=mesh, in_specs=in_specs, out_specs=out_specs, check_vma=False
    )
```

profile of v0, /device:TPU:1, one launch (start us, length us, event | category | flops | bytes accessed | tf_op | source)
XLA Modules:
  0.0 218.1 jit_solution(11876508315484006933)
XLA Ops:
  7.2 0.8 fusion.90
  8.1 0.2 select_reduce_fusion.1
  8.2 0.8 fusion.91
  9.2 0.7 sub.147
  9.8 6.3 %all-to-all-start = ((s32[8,1,5]{2,1,0:T(1,128)}), s32[8,1,5]{2,1,0:T(1,128)S(1)}, u32[]{:S(2)}, u32[]{:S(2)}) async-start(s32[8,1,5]{2,1,0:T(1,128)} %bitcast.19), calls=%async_computation | async-start | bytes 8192 | tf_op jit(solution)/shard_map/all_to_all | solution.py:127
  16.2 0.7 sqrt_bitcast_fusion
  16.9 0.3 fusion.75
  17.2 1.2 reshape.153
  18.4 5.0 %fusion.73 = f32[8,5,16384]{2,1,0:T(8,128)} fusion(f32[8,16384,1]{1,0,2:T(8,128)S(1)} %reshape.153, f32[8,5,8]{1,0,2:T(8,128)S(1)} %dot_general.16), kind=kOutput, calls=%fused_computation.120 | convolution fusion | flops 62914560 | bytes 3147008 | tf_op jit(solution)/shard_map/dot_general | solution.py:120
  23.4 5.6 %all-to-all-start.1 = ((f32[8,5,16384]{2,1,0:T(8,128)}), f32[8,5,16384]{2,1,0:T(8,128)}, u32[]{:S(2)}, u32[]{:S(2)}) async-start(f32[8,5,16384]{2,1,0:T(8,128)} %fusion.73), calls=%async_computation.1 | async-start | bytes 8388608 | tf_op jit(solution)/shard_map/all_to_all | solution.py:126
  29.0 0.6 fusion.118
  30.9 0.7 select_bitcast_fusion.1
  31.6 0.3 copy.85
  32.0 0.7 fusion.116
  32.6 1.0 fusion.110
  33.6 1.1 fusion.111
  34.8 0.7 fusion.117
  35.5 0.5 broadcast.320
  36.0 0.6 reduce.3
  36.6 110.9 %all-reduce.39.cloned.1.call-done = (f32[4,32,128]{2,1,0:T(8,128)}, f32[4,32,128]{2,1,0:T(8,128)}) async-done(((f32[4,32,128]{2,1,0:T(8,128)}, f32[4,32,128]{2,1,0:T(8,128)}), (f32[4,32,128]{2,1,0:T(8,128)}, f32[4,32,128]{2,1,0:T(8,128)})) %all-reduce.39.cloned.1.call-update) | async-done | bytes 131088 | tf_op jit(solution)/shard_map/psum | solution.py:15
  147.6 0.9 pad_maximum_fusion.11
  148.5 4.6 %collective-permute-start = (f32[11,1,32,128]{3,0,2,1:T(8,128)S(1)}, f32[11,1,32,128]{3,0,2,1:T(8,128)S(1)}, u32[]{:S(2)}, u32[]{:S(2)}) collective-permute-start(f32[11,1,32,128]{3,0,2,1:T(8,128)S(1)} %get-tuple-element.40), channel_id=1, source_target_pairs={{1,0},{2,1},{3,2},{5,4},{6,5},{7,6},{9,8},{10,9},{11,10},{13,12},{... | collective-permute-start | bytes 540680 | tf_op jit(solution)/shard_map/ppermute | solution.py:28
  153.1 3.0 %collective-permute-start.1 = (f32[11,1,32,128]{3,0,2,1:T(8,128)S(1)}, f32[11,1,32,128]{3,0,2,1:T(8,128)S(1)}, u32[]{:S(2)}, u32[]{:S(2)}) collective-permute-start(f32[11,1,32,128]{3,0,2,1:T(8,128)S(1)} %get-tuple-element.41), channel_id=1, source_target_pairs={{0,1},{1,2},{2,3},{4,5},{5,6},{6,7},{8,9},{9,10},{10,11},{12,13},{... | collective-permute-start | bytes 540680 | tf_op jit(solution)/shard_map/ppermute | solution.py:26
  156.3 0.8 add_multiply_fusion.3
  157.1 1.0 collective-permute-done
  158.2 1.0 fusion.68
  159.2 0.1 collective-permute-done.1
  159.4 1.0 fusion.67
  160.5 0.5 copy-done.13
  161.0 2.7 %reshape.152 = f32[40,16384]{1,0:T(8,128)S(1)} reshape(f32[8,5,16384]{2,1,0:T(8,128)} %all-to-all-done.1) | data formatting | bytes 5242880 | tf_op jit(solution)/shard_map/reshape | solution.py:129
  163.7 0.5 copy.118
  164.2 2.5 %fusion = f32[8,2,4,32,128]{4,0,3,2,1:T(8,128)S(1)} fusion(f32[4,32,128,40]{2,1,0,3:T(8,128)S(1)} %bitcast.97, s32[40]{0:T(128)S(1)} %eq.90, s32[8,2]{0,1:T(2,128)S(1)} %multiply_add_fusion), kind=kOutput, calls=%fused_computation | convolution fusion | flops 125829760 | bytes 3670240 | tf_op jit(solution)/shard_map/dot_general | solution.py:133
  166.7 4.4 %collective-permute-start.2 = (f32[8,2,1,32,128]{4,0,3,2,1:T(8,128)S(1)}, f32[8,2,1,32,128]{4,0,3,2,1:T(8,128)S(1)}, u32[]{:S(2)}, u32[]{:S(2)}) collective-permute-start(f32[8,2,1,32,128]{4,0,3,2,1:T(8,128)S(1)} %get-tuple-element.22), channel_id=1, source_target_pairs={{0,1},{1,2},{2,3},{4,5},{5,6},{6,7},{8,9},{9,10},{10,11},{12,13},{... | collective-permute-start | bytes 786440 | tf_op jit(solution)/shard_map/ppermute | solution.py:26
  171.1 2.1 collective-permute-start.3
  173.2 0.3 pad_maximum_fusion.1
  173.7 0.7 collective-permute-done.2
  174.4 4.6 %collective-permute-done.3 = f32[8,2,1,32,128]{4,0,3,2,1:T(8,128)S(1)} collective-permute-done((f32[8,2,1,32,128]{4,0,3,2,1:T(8,128)S(1)}, f32[8,2,1,32,128]{4,0,3,2,1:T(8,128)S(1)}, u32[]{:S(2)}, u32[]{:S(2)}) %collective-permute-start.3) | collective-permute-done | bytes 262176 | tf_op jit(solution)/shard_map/ppermute | solution.py:28
  179.5 0.3 fusion.98
  179.9 0.5 copy-done.4
  180.4 0.2 copy-done.5
  180.5 0.2 copy-done.6
  180.7 0.2 copy-done.7
  180.9 0.2 copy-done.8
  181.0 0.2 copy-done.15
  181.4 2.7 %broadcast_divide_fusion = (f32[8,4,32,128]{3,0,2,1:T(8,128)S(1)}, f32[8,4,32,128]{3,0,2,1:T(8,128)S(1)}) fusion(f32[4,32,128]{2,1,0:T(8,128)S(1)} %get-tuple-element.18, f32[8,4,32,127]{3,0,2,1:T(8,128)S(1)} %get-tuple-element.104, f32[4,32,128]{2,1,0:T(8,128)S(1)} %copy-done.17, f32[8,4,32,127]{3,0,2,1:T(8,128)S(1)} %get-tuple-element.105, ...), kind=kLoop, calls=%fused_computation.88 | loop fusion | flops 7471104 | bytes 13705216 | tf_op jit(solution)/shard_map/div | solution.py:145
  184.0 0.2 fusion.109
  184.3 1.9 collective-permute-start.4
  186.2 3.8 %collective-permute-start.5 = (f32[8,1,32,128]{3,0,2,1:T(8,128)S(1)}, f32[8,1,32,128]{3,0,2,1:T(8,128)S(1)}, u32[]{:S(2)}, u32[]{:S(2)}) collective-permute-start(f32[8,1,32,128]{3,0,2,1:T(8,128)S(1)} %get-tuple-element.55), channel_id=1, source_target_pairs={{0,1},{1,2},{2,3},{4,5},{5,6},{6,7},{8,9},{9,10},{10,11},{12,13},{... | collective-permute-start | bytes 393224 | tf_op jit(solution)/shard_map/ppermute | solution.py:26
  190.1 0.9 copy.110
  191.0 0.8 collective-permute-done.5
  191.8 0.5 divide_add_fusion.1
  192.3 0.2 fusion.106
  192.5 1.9 collective-permute-start.6
  194.5 4.4 %collective-permute-start.7 = (f32[8,1,32,128]{3,0,2,1:T(8,128)S(1)}, f32[8,1,32,128]{3,0,2,1:T(8,128)S(1)}, u32[]{:S(2)}, u32[]{:S(2)}) collective-permute-start(f32[8,1,32,128]{3,0,2,1:T(8,128)S(1)} %get-tuple-element.49), channel_id=1, source_target_pairs={{0,1},{1,2},{2,3},{4,5},{5,6},{6,7},{8,9},{9,10},{10,11},{12,13},{... | collective-permute-start | bytes 393224 | tf_op jit(solution)/shard_map/ppermute | solution.py:26
  198.9 0.6 collective-permute-done.6
  199.5 1.2 collective-permute-done.7
  200.7 0.6 divide_add_fusion
  201.3 0.2 fusion.102
  201.6 1.9 collective-permute-start.8
  203.5 4.4 %collective-permute-start.9 = (f32[8,1,32,128]{3,0,2,1:T(8,128)S(1)}, f32[8,1,32,128]{3,0,2,1:T(8,128)S(1)}, u32[]{:S(2)}, u32[]{:S(2)}) collective-permute-start(f32[8,1,32,128]{3,0,2,1:T(8,128)S(1)} %get-tuple-element.47), channel_id=1, source_target_pairs={{0,1},{1,2},{2,3},{4,5},{5,6},{6,7},{8,9},{9,10},{10,11},{12,13},{... | collective-permute-start | bytes 393224 | tf_op jit(solution)/shard_map/ppermute | solution.py:26
  207.9 0.6 collective-permute-done.8
  208.6 1.2 collective-permute-done.9
  209.8 0.6 fusion.15
  210.4 0.9 copy.111
  (90 shorter events, 1.7 us)
Async XLA Ops:
  9.8 13.6 %all-to-all-start = ((s32[8,1,5]{2,1,0:T(1,128)}), s32[8,1,5]{2,1,0:T(1,128)S(1)}, u32[]{:S(2)}, u32[]{:S(2)}) async-start(s32[8,1,5]{2,1,0:T(1,128)} %bitcast.19), calls=%async_computation | async-start | bytes 8192 | tf_op jit(solution)/shard_map/all_to_all | solution.py:127
  23.4 5.7 %copy-start.33 = (s32[2]{0:T(128)S(1)}, s32[2]{0:T(128)}, u32[]{:S(2)}) copy-start(s32[2]{0:T(128)} %param.10) | copy-start | bytes 28
  23.4 7.5 %copy-start.32 = (f32[1,4,32,128]{3,2,1,0:T(8,128)S(1)}, f32[1,4,32,128]{3,2,1,0:T(8,128)}, u32[]{:S(2)}) copy-start(f32[1,4,32,128]{3,2,1,0:T(8,128)} %param.9) | copy-start | bytes 196612
  23.4 8.2 %copy-start.3 = (f32[8,4,32,128]{3,2,1,0:T(8,128)S(1)}, f32[8,4,32,128]{3,2,1,0:T(8,128)}, u32[]{:S(2)}) copy-start(f32[8,4,32,128]{3,2,1,0:T(8,128)} %param.6) | copy-start | bytes 1572868
  23.4 137.6 %all-to-all-start.1 = ((f32[8,5,16384]{2,1,0:T(8,128)}), f32[8,5,16384]{2,1,0:T(8,128)}, u32[]{:S(2)}, u32[]{:S(2)}) async-start(f32[8,5,16384]{2,1,0:T(8,128)} %fusion.73), calls=%async_computation.1 | async-start | bytes 8388608 | tf_op jit(solution)/shard_map/all_to_all | solution.py:126
  29.0 3.0 %copy-start = (f32[4,32,128]{2,1,0:T(8,128)S(1)}, f32[4,32,128]{2,1,0:T(8,128)}, u32[]{:S(2)}) copy-start(f32[4,32,128]{2,1,0:T(8,128)} %param.8) | copy-start | bytes 196612
  29.0 118.6 %all-reduce.39.cloned.1.call-start = ((), (), s32[]{:S(2)}) async-start(), calls=%async_computation.2 | async-start | bytes 262144 | tf_op jit(solution)/shard_map/psum | solution.py:15
  147.6 8.5 %copy-start.2 = (f32[4,32,128]{2,1,0:T(8,128)S(1)}, f32[4,32,128]{2,1,0:T(8,128)}, u32[]{:S(2)}) copy-start(f32[4,32,128]{2,1,0:T(8,128)} %get-tuple-element.11) | copy-start | bytes 196612
  147.6 8.6 %copy-start.1 = (f32[4,32,128]{2,1,0:T(8,128)S(1)}, f32[4,32,128]{2,1,0:T(8,128)}, u32[]{:S(2)}) copy-start(f32[4,32,128]{2,1,0:T(8,128)} %get-tuple-element.10) | copy-start | bytes 196612
  148.5 9.7 %collective-permute-start = (f32[11,1,32,128]{3,0,2,1:T(8,128)S(1)}, f32[11,1,32,128]{3,0,2,1:T(8,128)S(1)}, u32[]{:S(2)}, u32[]{:S(2)}) collective-permute-start(f32[11,1,32,128]{3,0,2,1:T(8,128)S(1)} %get-tuple-element.40), channel_id=1, source_target_pairs={{1,0},{2,1},{3,2},{5,4},{6,5},{7,6},{9,8},{10,9},{11,10},{13,12},{... | collective-permute-start | bytes 540680 | tf_op jit(solution)/shard_map/ppermute | solution.py:28
  153.1 6.3 %collective-permute-start.1 = (f32[11,1,32,128]{3,0,2,1:T(8,128)S(1)}, f32[11,1,32,128]{3,0,2,1:T(8,128)S(1)}, u32[]{:S(2)}, u32[]{:S(2)}) collective-permute-start(f32[11,1,32,128]{3,0,2,1:T(8,128)S(1)} %get-tuple-element.41), channel_id=1, source_target_pairs={{0,1},{1,2},{2,3},{4,5},{5,6},{6,7},{8,9},{9,10},{10,11},{12,13},{... | collective-permute-start | bytes 540680 | tf_op jit(solution)/shard_map/ppermute | solution.py:26
  158.2 2.3 %copy-start.9 = (f32[11,1,32,128]{3,0,2,1:T(8,128)}, f32[11,1,32,128]{3,0,2,1:T(8,128)S(1)}, u32[]{:S(2)}) copy-start(f32[11,1,32,128]{3,0,2,1:T(8,128)S(1)} %collective-permute-done) | copy-start | bytes 540676
  159.4 1.1 copy-start.11
  160.4 0.6 copy-start.13
  164.2 9.0 %copy-start.10 = (f32[11,1,32,128]{3,0,2,1:T(8,128)S(1)}, f32[11,1,32,128]{3,0,2,1:T(8,128)}, u32[]{:S(2)}) copy-start(f32[11,1,32,128]{3,0,2,1:T(8,128)} %copy-done.9) | copy-start | bytes 540676
  164.2 9.0 %copy-start.12 = (f32[11,1,32,128]{3,0,2,1:T(8,128)S(1)}, f32[11,1,32,128]{3,0,2,1:T(8,128)}, u32[]{:S(2)}) copy-start(f32[11,1,32,128]{3,0,2,1:T(8,128)} %copy-done.11) | copy-start | bytes 540676
  166.7 7.7 %collective-permute-start.2 = (f32[8,2,1,32,128]{4,0,3,2,1:T(8,128)S(1)}, f32[8,2,1,32,128]{4,0,3,2,1:T(8,128)S(1)}, u32[]{:S(2)}, u32[]{:S(2)}) collective-permute-start(f32[8,2,1,32,128]{4,0,3,2,1:T(8,128)S(1)} %get-tuple-element.22), channel_id=1, source_target_pairs={{0,1},{1,2},{2,3},{4,5},{5,6},{6,7},{8,9},{9,10},{10,11},{12,13},{... | collective-permute-start | bytes 786440 | tf_op jit(solution)/shard_map/ppermute | solution.py:26
  171.1 2.4 %copy-start.14 = (f32[1,4,32,128]{3,0,2,1:T(1,128)S(1)}, f32[1,4,32,128]{3,0,2,1:T(1,128)}, u32[]{:S(2)}) copy-start(f32[1,4,32,128]{3,0,2,1:T(1,128)} %copy-done.13) | copy-start | bytes 196612
  171.1 2.4 %copy-start.28 = (f32[4,31,128]{2,1,0:T(8,128)S(1)}, f32[4,31,128]{2,1,0:T(8,128)}, u32[]{:S(2)}) copy-start(f32[4,31,128]{2,1,0:T(8,128)} %get-tuple-element.88) | copy-start | bytes 190468
  171.1 2.4 %copy-start.29 = (f32[4,31,128]{2,1,0:T(8,128)S(1)}, f32[4,31,128]{2,1,0:T(8,128)}, u32[]{:S(2)}) copy-start(f32[4,31,128]{2,1,0:T(8,128)} %get-tuple-element.89) | copy-start | bytes 190468
  171.1 2.4 %copy-start.30 = (f32[4,32,127]{2,1,0:T(8,128)S(1)}, f32[4,32,127]{2,1,0:T(8,128)}, u32[]{:S(2)}) copy-start(f32[4,32,127]{2,1,0:T(8,128)} %get-tuple-element.90) | copy-start | bytes 195076
  171.1 2.4 %copy-start.31 = (f32[4,32,127]{2,1,0:T(8,128)S(1)}, f32[4,32,127]{2,1,0:T(8,128)}, u32[]{:S(2)}) copy-start(f32[4,32,127]{2,1,0:T(8,128)} %get-tuple-element.91) | copy-start | bytes 195076
  171.1 7.8 %collective-permute-start.3 = (f32[8,2,1,32,128]{4,0,3,2,1:T(8,128)S(1)}, f32[8,2,1,32,128]{4,0,3,2,1:T(8,128)S(1)}, u32[]{:S(2)}, u32[]{:S(2)}) collective-permute-start(f32[8,2,1,32,128]{4,0,3,2,1:T(8,128)S(1)} %get-tuple-element.23), channel_id=1, source_target_pairs={{1,0},{2,1},{3,2},{5,4},{6,5},{7,6},{9,8},{10,9},{11,10},{13,12},{... | collective-permute-start | bytes 786440 | tf_op jit(solution)/shard_map/ppermute | solution.py:28
  179.3 1.0 copy-start.4
  179.3 1.2 copy-start.5
  179.4 1.3 copy-start.6
  179.4 1.5 copy-start.7
  179.4 1.6 copy-start.8
  179.4 1.8 copy-start.15
  179.4 1.8 copy-start.16
  179.4 1.8 copy-start.17
  179.4 1.8 copy-start.18
  179.4 1.7 copy-start.19
  179.4 1.8 copy-start.20
  179.5 1.8 copy-start.21
  179.5 1.8 copy-start.22
  179.5 1.8 copy-start.23
  179.5 1.8 copy-start.24
  179.5 1.8 copy-start.25
  179.5 1.8 copy-start.26
  179.5 1.8 copy-start.27
  184.3 6.7 %collective-permute-start.4 = (f32[8,1,32,128]{3,0,2,1:T(8,128)S(1)}, f32[8,1,32,128]{3,0,2,1:T(8,128)S(1)}, u32[]{:S(2)}, u32[]{:S(2)}) collective-permute-start(f32[8,1,32,128]{3,0,2,1:T(8,128)S(1)} %get-tuple-element.54), channel_id=1, source_target_pairs={{1,0},{2,1},{3,2},{5,4},{6,5},{7,6},{9,8},{10,9},{11,10},{13,12},{... | collective-permute-start | bytes 393224 | tf_op jit(solution)/shard_map/ppermute | solution.py:28
  186.2 5.6 %collective-permute-start.5 = (f32[8,1,32,128]{3,0,2,1:T(8,128)S(1)}, f32[8,1,32,128]{3,0,2,1:T(8,128)S(1)}, u32[]{:S(2)}, u32[]{:S(2)}) collective-permute-start(f32[8,1,32,128]{3,0,2,1:T(8,128)S(1)} %get-tuple-element.55), channel_id=1, source_target_pairs={{0,1},{1,2},{2,3},{4,5},{5,6},{6,7},{8,9},{9,10},{10,11},{12,13},{... | collective-permute-start | bytes 393224 | tf_op jit(solution)/shard_map/ppermute | solution.py:26
  192.5 7.0 %collective-permute-start.6 = (f32[8,1,32,128]{3,0,2,1:T(8,128)S(1)}, f32[8,1,32,128]{3,0,2,1:T(8,128)S(1)}, u32[]{:S(2)}, u32[]{:S(2)}) collective-permute-start(f32[8,1,32,128]{3,0,2,1:T(8,128)S(1)} %get-tuple-element.48), channel_id=1, source_target_pairs={{1,0},{2,1},{3,2},{5,4},{6,5},{7,6},{9,8},{10,9},{11,10},{13,12},{... | collective-permute-start | bytes 393224 | tf_op jit(solution)/shard_map/ppermute | solution.py:28
  194.5 6.3 %collective-permute-start.7 = (f32[8,1,32,128]{3,0,2,1:T(8,128)S(1)}, f32[8,1,32,128]{3,0,2,1:T(8,128)S(1)}, u32[]{:S(2)}, u32[]{:S(2)}) collective-permute-start(f32[8,1,32,128]{3,0,2,1:T(8,128)S(1)} %get-tuple-element.49), channel_id=1, source_target_pairs={{0,1},{1,2},{2,3},{4,5},{5,6},{6,7},{8,9},{9,10},{10,11},{12,13},{... | collective-permute-start | bytes 393224 | tf_op jit(solution)/shard_map/ppermute | solution.py:26
  201.6 7.0 %collective-permute-start.8 = (f32[8,1,32,128]{3,0,2,1:T(8,128)S(1)}, f32[8,1,32,128]{3,0,2,1:T(8,128)S(1)}, u32[]{:S(2)}, u32[]{:S(2)}) collective-permute-start(f32[8,1,32,128]{3,0,2,1:T(8,128)S(1)} %get-tuple-element.46), channel_id=1, source_target_pairs={{1,0},{2,1},{3,2},{5,4},{6,5},{7,6},{9,8},{10,9},{11,10},{13,12},{... | collective-permute-start | bytes 393224 | tf_op jit(solution)/shard_map/ppermute | solution.py:28
  203.5 6.3 %collective-permute-start.9 = (f32[8,1,32,128]{3,0,2,1:T(8,128)S(1)}, f32[8,1,32,128]{3,0,2,1:T(8,128)S(1)}, u32[]{:S(2)}, u32[]{:S(2)}) collective-permute-start(f32[8,1,32,128]{3,0,2,1:T(8,128)S(1)} %get-tuple-element.47), channel_id=1, source_target_pairs={{0,1},{1,2},{2,3},{4,5},{5,6},{6,7},{8,9},{9,10},{10,11},{12,13},{... | collective-permute-start | bytes 393224 | tf_op jit(solution)/shard_map/ppermute | solution.py:26
Sparse Core Ops, SparseCore 0:
  33.2 114.2 all-reduce.38
where the time goes:
time: 219 us; the launch traced here: 218 us
  waiting for transfers between devices  122 us (56%)
  starting transfers between devices  44.3 us (20%)
  between operations  15.9 us (7%)
  local copies, waits for them, and re-layouts  15.6 us (7%)
  other arithmetic  12.7 us (6%)
  matrix products  7.73 us (4%)
    psum x1, waiting for transfers between devices, spread(): return lax.psum(jnp.where(mine, array, jnp.zeros_like(array)), axis)  111 us
    ppermute x5, starting transfers between devices, extended_2(): lax.ppermute(tail, axis, [(i, (i + 1) % count) for i in range(ends)])  19.9 us
    ppermute x5, starting transfers between devices, extended_2(): lax.ppermute(head, axis, [((i + 1) % count, i) for i in range(ends)])  12.4 us
    ppermute x5, waiting for transfers between devices, extended_2(): lax.ppermute(head, axis, [((i + 1) % count, i) for i in range(ends)])  6.89 us
    all_to_all x1, starting transfers between devices, per_device(): lax.all_to_all(slot_ids, 'chaos', split_axis=0, concat_axis=0, tiled=True)  6.34 us
    all_to_all x1, starting transfers between devices, per_device(): lax.all_to_all(send_block, 'chaos', split_axis=0, concat_axis=0, tiled=True)  5.58 us
    dot_general x1, matrix products, per_device(): send_block = jnp.dot(send_matrix, payload, precision=lax.Precision.HIGHEST)  5.01 us
    slice x16, local copies, waits for them, and re-layouts, neighbour(): lax.slice_in_dim(values, 1, length, axis=along_axis)  4.97 us
  transfers between devices with their start and end apart: 13, of which 10 were waited for; matrix products, arithmetic and copies ran while one was open for 9% of the time, Pallas kernels for 0%

commit v1 on v0

--- a/solution.py
+++ b/solution.py
@@ -12,7 +12,7 @@
 
 def spread(array, axis, root):
     mine = lax.axis_index(axis) == root
-    return lax.psum(jnp.where(mine, array, jnp.zeros_like(array)), axis)
+    return jnp.sum(lax.all_gather(jnp.where(mine, array, jnp.zeros_like(array)), axis), axis=0)
 
 
 def extended_2(cells, sides, width):

time: 219 us -> 233 us (1.064)
  blocking collectives: 0 us -> 133 us
  waiting for transfers between devices: 122 us -> 9.78 us
  between operations: 15.9 us -> 2.56 us
  starting transfers between devices: 44.3 us -> 50.9 us
    all_gather x0 -> x2, blocking collectives: none -> 133 us  [spread(): lax.all_gather(jnp.where(mine, array, jnp.zeros_like(array)), axis)]
    psum x1 -> x0, waiting for transfers between devices: 111 us -> none  [spread(): return lax.psum(jnp.where(mine, array, jnp.zeros_like(array)), axis)]
    ppermute x5, starting transfers between devices: 12.4 us -> 21 us  [extended_2(): lax.ppermute(head, axis, [((i + 1) % count, i) for i in range(ends)])]
    unnamed x72 -> x68, local copies, waits for them, and re-layouts: 4.67 us -> 4.68 us
  transfers between devices with their start and end apart: 13 -> 12, of which waited for: 10 -> 7; matrix products, arithmetic and copies ran while one was open for 9% -> 8% of each run, Pallas kernels for 0% -> 0%
where the time goes in v1:
time: 233 us; the launch traced here: 232 us
  blocking collectives  133 us (57%)
  starting transfers between devices  50.9 us (22%)
  local copies, waits for them, and re-layouts  15.7 us (7%)
  other arithmetic  12.1 us (5%)
  waiting for transfers between devices  9.78 us (4%)
  matrix products  7.74 us (3%)
  between operations  2.56 us (1%)
    all_gather x2, blocking collectives, spread(): lax.all_gather(jnp.where(mine, array, jnp.zeros_like(array)), axis)  133 us
    ppermute x5, starting transfers between devices, extended_2(): lax.ppermute(head, axis, [((i + 1) % count, i) for i in range(ends)])  21 us
    ppermute x5, starting transfers between devices, extended_2(): lax.ppermute(tail, axis, [(i, (i + 1) % count) for i in range(ends)])  18 us
    all_to_all x1, starting transfers between devices, per_device(): lax.all_to_all(slot_ids, 'chaos', split_axis=0, concat_axis=0, tiled=True)  6.34 us
    ppermute x5, waiting for transfers between devices, extended_2(): lax.ppermute(head, axis, [((i + 1) % count, i) for i in range(ends)])  5.85 us
    all_to_all x1, starting transfers between devices, per_device(): lax.all_to_all(send_block, 'chaos', split_axis=0, concat_axis=0, tiled=True)  5.58 us
    dot_general x1, matrix products, per_device(): send_block = jnp.dot(send_matrix, payload, precision=lax.Precision.HIGHEST)  5.01 us
    slice x16, local copies, waits for them, and re-layouts, neighbour(): lax.slice_in_dim(values, 1, length, axis=along_axis)  4.99 us
  transfers between devices with their start and end apart: 12, of which 7 were waited for; matrix products, arithmetic and copies ran while one was open for 8% of the time, Pallas kernels for 0%

profile of v1, /device:TPU:1, one launch (start us, length us, event | category | flops | bytes accessed | tf_op | source)
XLA Modules:
  0.0 231.8 jit_solution(4399578458173283218)
XLA Ops:
  0.6 0.8 fusion.90
  1.5 0.2 select_reduce_fusion.1
  1.7 0.8 fusion.91
  2.6 0.7 sub.147
  3.3 6.3 %all-to-all-start = ((s32[8,1,5]{2,1,0:T(1,128)}), s32[8,1,5]{2,1,0:T(1,128)S(1)}, u32[]{:S(2)}, u32[]{:S(2)}) async-start(s32[8,1,5]{2,1,0:T(1,128)} %bitcast.17), calls=%async_computation | async-start | bytes 8192 | tf_op jit(solution)/shard_map/all_to_all | solution.py:127
  9.6 0.7 sqrt_bitcast_fusion
  10.3 0.3 fusion.75
  10.7 1.2 reshape.147
  11.8 5.0 %fusion.73 = f32[8,5,16384]{2,1,0:T(8,128)} fusion(f32[8,16384,1]{1,0,2:T(8,128)S(1)} %reshape.147, f32[8,5,8]{1,0,2:T(8,128)S(1)} %dot_general.16), kind=kOutput, calls=%fused_computation.118 | convolution fusion | flops 62914560 | bytes 3147008 | tf_op jit(solution)/shard_map/dot_general | solution.py:120
  16.9 5.6 %all-to-all-start.1 = ((f32[8,5,16384]{2,1,0:T(8,128)}), f32[8,5,16384]{2,1,0:T(8,128)}, u32[]{:S(2)}, u32[]{:S(2)}) async-start(f32[8,5,16384]{2,1,0:T(8,128)} %fusion.73), calls=%async_computation.1 | async-start | bytes 8388608 | tf_op jit(solution)/shard_map/all_to_all | solution.py:126
  22.4 0.3 copy.85
  22.8 0.6 fusion.118
  24.7 107.6 %all_gather.8 = f32[8,4,32,128]{3,2,1,0:T(8,128)S(1)} all-gather(f32[1,4,32,128]{3,2,1,0:T(8,128)S(1)} %get-tuple-element.84), channel_id=1, replica_groups=mesh['chaos'=8,'space'=4] {'chaos'}, dimensions={0}, use_global_device_ids=true | all-gather | bytes 589824 | tf_op jit(solution)/shard_map/all_gather | solution.py:15
  132.3 25.5 %all_gather.9 = f32[8,4,32,128]{3,2,1,0:T(8,128)S(1)} all-gather(f32[1,4,32,128]{3,2,1,0:T(8,128)S(1)} %get-tuple-element.85), channel_id=1, replica_groups=mesh['chaos'=8,'space'=4] {'chaos'}, dimensions={0}, use_global_device_ids=true | all-gather | bytes 589824 | tf_op jit(solution)/shard_map/all_gather | solution.py:15
  158.0 13.2 %collective-permute-start = (f32[11,1,32,128]{3,0,2,1:T(8,128)S(1)}, f32[11,1,32,128]{3,0,2,1:T(8,128)S(1)}, u32[]{:S(2)}, u32[]{:S(2)}) collective-permute-start(f32[11,1,32,128]{3,0,2,1:T(8,128)S(1)} %get-tuple-element.38), channel_id=1, source_target_pairs={{1,0},{2,1},{3,2},{5,4},{6,5},{7,6},{9,8},{10,9},{11,10},{13,12},{... | collective-permute-start | bytes 540680 | tf_op jit(solution)/shard_map/ppermute | solution.py:28
  171.2 3.0 %collective-permute-start.1 = (f32[11,1,32,128]{3,0,2,1:T(8,128)S(1)}, f32[11,1,32,128]{3,0,2,1:T(8,128)S(1)}, u32[]{:S(2)}, u32[]{:S(2)}) collective-permute-start(f32[11,1,32,128]{3,0,2,1:T(8,128)S(1)} %get-tuple-element.39), channel_id=1, source_target_pairs={{0,1},{1,2},{2,3},{4,5},{5,6},{6,7},{8,9},{9,10},{10,11},{12,13},{... | collective-permute-start | bytes 540680 | tf_op jit(solution)/shard_map/ppermute | solution.py:26
  174.3 0.7 fusion.116
  175.1 0.8 add_multiply_fusion.7
  175.9 0.8 add_multiply_fusion.3
  176.6 1.0 fusion.110
  177.7 1.1 fusion.111
  178.8 0.7 fusion.117
  179.5 0.5 broadcast.317
  180.0 0.6 reduce.3
  180.8 1.1 fusion.68
  181.8 1.0 fusion.67
  183.0 0.5 copy-done.11
  183.5 2.7 %reshape.146 = f32[40,16384]{1,0:T(8,128)S(1)} reshape(f32[8,5,16384]{2,1,0:T(8,128)} %all-to-all-done.1) | data formatting | bytes 5242880 | tf_op jit(solution)/shard_map/reshape | solution.py:129
  186.2 0.5 copy.118
  186.7 2.5 %fusion = f32[8,2,4,32,128]{4,0,3,2,1:T(8,128)S(1)} fusion(f32[4,32,128,40]{2,1,0,3:T(8,128)S(1)} %bitcast.93, s32[40]{0:T(128)S(1)} %eq.90, s32[8,2]{0,1:T(2,128)S(1)} %multiply_add_fusion), kind=kOutput, calls=%fused_computation | convolution fusion | flops 125829760 | bytes 3670240 | tf_op jit(solution)/shard_map/dot_general | solution.py:133
  189.2 2.4 %collective-permute-start.2 = (f32[8,2,1,32,128]{4,0,3,2,1:T(8,128)S(1)}, f32[8,2,1,32,128]{4,0,3,2,1:T(8,128)S(1)}, u32[]{:S(2)}, u32[]{:S(2)}) collective-permute-start(f32[8,2,1,32,128]{4,0,3,2,1:T(8,128)S(1)} %get-tuple-element.20), channel_id=1, source_target_pairs={{0,1},{1,2},{2,3},{4,5},{5,6},{6,7},{8,9},{9,10},{10,11},{12,13},{... | collective-permute-start | bytes 786440 | tf_op jit(solution)/shard_map/ppermute | solution.py:26
  191.7 2.1 collective-permute-start.3
  193.8 0.3 pad_maximum_fusion.1
  194.2 0.7 collective-permute-done.2
  194.9 4.6 %collective-permute-done.3 = f32[8,2,1,32,128]{4,0,3,2,1:T(8,128)S(1)} collective-permute-done((f32[8,2,1,32,128]{4,0,3,2,1:T(8,128)S(1)}, f32[8,2,1,32,128]{4,0,3,2,1:T(8,128)S(1)}, u32[]{:S(2)}, u32[]{:S(2)}) %collective-permute-start.3) | collective-permute-done | bytes 262176 | tf_op jit(solution)/shard_map/ppermute | solution.py:28
  199.6 0.1 slice_bitcast_fusion.1
  199.7 0.1 fusion.97
  200.1 0.3 fusion.98
  200.4 0.5 copy-done.2
  200.9 0.2 copy-done.3
  201.1 0.2 copy-done.4
  201.2 0.2 copy-done.5
  201.4 0.2 copy-done.6
  201.6 0.2 copy-done.13
  201.9 2.7 %broadcast_divide_fusion = (f32[8,4,32,128]{3,0,2,1:T(8,128)S(1)}, f32[8,4,32,128]{3,0,2,1:T(8,128)S(1)}) fusion(f32[4,32,128]{2,1,0:T(8,128)S(1)} %get-tuple-element.16, f32[8,4,32,127]{3,0,2,1:T(8,128)S(1)} %get-tuple-element.98, f32[4,32,128]{2,1,0:T(8,128)S(1)} %copy-done.19, f32[8,4,32,127]{3,0,2,1:T(8,128)S(1)} %get-tuple-element.99, ...), kind=kLoop, calls=%fused_computation.88 | loop fusion | flops 7471104 | bytes 13705216 | tf_op jit(solution)/shard_map/div | solution.py:145
  204.6 0.2 fusion.109
  204.8 1.9 collective-permute-start.4
  206.7 3.8 %collective-permute-start.5 = (f32[8,1,32,128]{3,0,2,1:T(8,128)S(1)}, f32[8,1,32,128]{3,0,2,1:T(8,128)S(1)}, u32[]{:S(2)}, u32[]{:S(2)}) collective-permute-start(f32[8,1,32,128]{3,0,2,1:T(8,128)S(1)} %get-tuple-element.53), channel_id=1, source_target_pairs={{0,1},{1,2},{2,3},{4,5},{5,6},{6,7},{8,9},{9,10},{10,11},{12,13},{... | collective-permute-start | bytes 393224 | tf_op jit(solution)/shard_map/ppermute | solution.py:26
  210.6 0.9 copy.110
  211.5 0.8 collective-permute-done.5
  212.3 0.5 divide_add_fusion.1
  212.8 0.2 fusion.106
  213.1 1.9 collective-permute-start.6
  215.0 4.4 %collective-permute-start.7 = (f32[8,1,32,128]{3,0,2,1:T(8,128)S(1)}, f32[8,1,32,128]{3,0,2,1:T(8,128)S(1)}, u32[]{:S(2)}, u32[]{:S(2)}) collective-permute-start(f32[8,1,32,128]{3,0,2,1:T(8,128)S(1)} %get-tuple-element.47), channel_id=1, source_target_pairs={{0,1},{1,2},{2,3},{4,5},{5,6},{6,7},{8,9},{9,10},{10,11},{12,13},{... | collective-permute-start | bytes 393224 | tf_op jit(solution)/shard_map/ppermute | solution.py:26
  219.4 0.6 collective-permute-done.6
  220.1 1.2 collective-permute-done.7
  221.3 0.6 divide_add_fusion
  221.9 0.2 fusion.102
  222.1 1.9 collective-permute-start.8
  224.0 4.4 %collective-permute-start.9 = (f32[8,1,32,128]{3,0,2,1:T(8,128)S(1)}, f32[8,1,32,128]{3,0,2,1:T(8,128)S(1)}, u32[]{:S(2)}, u32[]{:S(2)}) collective-permute-start(f32[8,1,32,128]{3,0,2,1:T(8,128)S(1)} %get-tuple-element.45), channel_id=1, source_target_pairs={{0,1},{1,2},{2,3},{4,5},{5,6},{6,7},{8,9},{9,10},{10,11},{12,13},{... | collective-permute-start | bytes 393224 | tf_op jit(solution)/shard_map/ppermute | solution.py:26
  228.5 0.6 collective-permute-done.8
  229.1 1.2 collective-permute-done.9
  230.3 0.6 fusion.15
  230.9 0.9 copy.111
  (88 shorter events, 1.6 us)
Async XLA Ops:
  3.3 13.6 %all-to-all-start = ((s32[8,1,5]{2,1,0:T(1,128)}), s32[8,1,5]{2,1,0:T(1,128)S(1)}, u32[]{:S(2)}, u32[]{:S(2)}) async-start(s32[8,1,5]{2,1,0:T(1,128)} %bitcast.17), calls=%async_computation | async-start | bytes 8192 | tf_op jit(solution)/shard_map/all_to_all | solution.py:127
  16.9 5.6 %copy-start.1 = (f32[8,4,32,128]{3,2,1,0:T(8,128)S(1)}, f32[8,4,32,128]{3,2,1,0:T(8,128)}, u32[]{:S(2)}) copy-start(f32[8,4,32,128]{3,2,1,0:T(8,128)} %param.6) | copy-start | bytes 1572868
  16.9 5.9 %copy-start.31 = (s32[2]{0:T(128)S(1)}, s32[2]{0:T(128)}, u32[]{:S(2)}) copy-start(s32[2]{0:T(128)} %param.10) | copy-start | bytes 28
  16.9 7.8 %copy-start.30 = (f32[1,4,32,128]{3,2,1,0:T(8,128)S(1)}, f32[1,4,32,128]{3,2,1,0:T(8,128)}, u32[]{:S(2)}) copy-start(f32[1,4,32,128]{3,2,1,0:T(8,128)} %param.9) | copy-start | bytes 196612
  16.9 166.7 %all-to-all-start.1 = ((f32[8,5,16384]{2,1,0:T(8,128)}), f32[8,5,16384]{2,1,0:T(8,128)}, u32[]{:S(2)}, u32[]{:S(2)}) async-start(f32[8,5,16384]{2,1,0:T(8,128)} %fusion.73), calls=%async_computation.1 | async-start | bytes 8388608 | tf_op jit(solution)/shard_map/all_to_all | solution.py:126
  22.8 135.1 %copy-start = (f32[4,32,128]{2,1,0:T(8,128)S(1)}, f32[4,32,128]{2,1,0:T(8,128)}, u32[]{:S(2)}) copy-start(f32[4,32,128]{2,1,0:T(8,128)} %param.8) | copy-start | bytes 196612
  158.0 22.8 %collective-permute-start = (f32[11,1,32,128]{3,0,2,1:T(8,128)S(1)}, f32[11,1,32,128]{3,0,2,1:T(8,128)S(1)}, u32[]{:S(2)}, u32[]{:S(2)}) collective-permute-start(f32[11,1,32,128]{3,0,2,1:T(8,128)S(1)} %get-tuple-element.38), channel_id=1, source_target_pairs={{1,0},{2,1},{3,2},{5,4},{6,5},{7,6},{9,8},{10,9},{11,10},{13,12},{... | collective-permute-start | bytes 540680 | tf_op jit(solution)/shard_map/ppermute | solution.py:28
  171.2 10.6 %collective-permute-start.1 = (f32[11,1,32,128]{3,0,2,1:T(8,128)S(1)}, f32[11,1,32,128]{3,0,2,1:T(8,128)S(1)}, u32[]{:S(2)}, u32[]{:S(2)}) collective-permute-start(f32[11,1,32,128]{3,0,2,1:T(8,128)S(1)} %get-tuple-element.39), channel_id=1, source_target_pairs={{0,1},{1,2},{2,3},{4,5},{5,6},{6,7},{8,9},{9,10},{10,11},{12,13},{... | collective-permute-start | bytes 540680 | tf_op jit(solution)/shard_map/ppermute | solution.py:26
  180.8 2.2 copy-start.7
  181.8 1.1 copy-start.9
  182.9 0.6 copy-start.11
  186.7 7.1 %copy-start.8 = (f32[11,1,32,128]{3,0,2,1:T(8,128)S(1)}, f32[11,1,32,128]{3,0,2,1:T(8,128)}, u32[]{:S(2)}) copy-start(f32[11,1,32,128]{3,0,2,1:T(8,128)} %copy-done.7) | copy-start | bytes 540676
  186.7 7.1 %copy-start.10 = (f32[11,1,32,128]{3,0,2,1:T(8,128)S(1)}, f32[11,1,32,128]{3,0,2,1:T(8,128)}, u32[]{:S(2)}) copy-start(f32[11,1,32,128]{3,0,2,1:T(8,128)} %copy-done.9) | copy-start | bytes 540676
  189.2 5.7 %collective-permute-start.2 = (f32[8,2,1,32,128]{4,0,3,2,1:T(8,128)S(1)}, f32[8,2,1,32,128]{4,0,3,2,1:T(8,128)S(1)}, u32[]{:S(2)}, u32[]{:S(2)}) collective-permute-start(f32[8,2,1,32,128]{4,0,3,2,1:T(8,128)S(1)} %get-tuple-element.20), channel_id=1, source_target_pairs={{0,1},{1,2},{2,3},{4,5},{5,6},{6,7},{8,9},{9,10},{10,11},{12,13},{... | collective-permute-start | bytes 786440 | tf_op jit(solution)/shard_map/ppermute | solution.py:26
  191.6 2.4 %copy-start.12 = (f32[1,4,32,128]{3,0,2,1:T(1,128)S(1)}, f32[1,4,32,128]{3,0,2,1:T(1,128)}, u32[]{:S(2)}) copy-start(f32[1,4,32,128]{3,0,2,1:T(1,128)} %copy-done.11) | copy-start | bytes 196612
  191.6 2.4 %copy-start.26 = (f32[4,31,128]{2,1,0:T(8,128)S(1)}, f32[4,31,128]{2,1,0:T(8,128)}, u32[]{:S(2)}) copy-start(f32[4,31,128]{2,1,0:T(8,128)} %get-tuple-element.86) | copy-start | bytes 190468
  191.6 2.4 %copy-start.27 = (f32[4,31,128]{2,1,0:T(8,128)S(1)}, f32[4,31,128]{2,1,0:T(8,128)}, u32[]{:S(2)}) copy-start(f32[4,31,128]{2,1,0:T(8,128)} %get-tuple-element.87) | copy-start | bytes 190468
  191.7 2.4 %copy-start.28 = (f32[4,32,127]{2,1,0:T(8,128)S(1)}, f32[4,32,127]{2,1,0:T(8,128)}, u32[]{:S(2)}) copy-start(f32[4,32,127]{2,1,0:T(8,128)} %get-tuple-element.88) | copy-start | bytes 195076
  191.7 2.4 %copy-start.29 = (f32[4,32,127]{2,1,0:T(8,128)S(1)}, f32[4,32,127]{2,1,0:T(8,128)}, u32[]{:S(2)}) copy-start(f32[4,32,127]{2,1,0:T(8,128)} %get-tuple-element.89) | copy-start | bytes 195076
  191.7 7.8 %collective-permute-start.3 = (f32[8,2,1,32,128]{4,0,3,2,1:T(8,128)S(1)}, f32[8,2,1,32,128]{4,0,3,2,1:T(8,128)S(1)}, u32[]{:S(2)}, u32[]{:S(2)}) collective-permute-start(f32[8,2,1,32,128]{4,0,3,2,1:T(8,128)S(1)} %get-tuple-element.21), channel_id=1, source_target_pairs={{1,0},{2,1},{3,2},{5,4},{6,5},{7,6},{9,8},{10,9},{11,10},{13,12},{... | collective-permute-start | bytes 786440 | tf_op jit(solution)/shard_map/ppermute | solution.py:28
  199.9 1.0 copy-start.2
  199.9 1.2 copy-start.3
  199.9 1.3 copy-start.4
  199.9 1.5 copy-start.5
  199.9 1.6 copy-start.6
  199.9 1.8 copy-start.13
  199.9 1.8 copy-start.14
  200.0 1.8 copy-start.15
  200.0 1.8 copy-start.16
  200.0 1.7 copy-start.17
  200.0 1.8 copy-start.18
  200.0 1.8 copy-start.19
  200.0 1.8 copy-start.20
  200.0 1.8 copy-start.21
  200.0 1.8 copy-start.22
  200.0 1.8 copy-start.23
  200.0 1.8 copy-start.24
  200.1 1.8 copy-start.25
  204.8 6.7 %collective-permute-start.4 = (f32[8,1,32,128]{3,0,2,1:T(8,128)S(1)}, f32[8,1,32,128]{3,0,2,1:T(8,128)S(1)}, u32[]{:S(2)}, u32[]{:S(2)}) collective-permute-start(f32[8,1,32,128]{3,0,2,1:T(8,128)S(1)} %get-tuple-element.52), channel_id=1, source_target_pairs={{1,0},{2,1},{3,2},{5,4},{6,5},{7,6},{9,8},{10,9},{11,10},{13,12},{... | collective-permute-start | bytes 393224 | tf_op jit(solution)/shard_map/ppermute | solution.py:28
  206.7 5.6 %collective-permute-start.5 = (f32[8,1,32,128]{3,0,2,1:T(8,128)S(1)}, f32[8,1,32,128]{3,0,2,1:T(8,128)S(1)}, u32[]{:S(2)}, u32[]{:S(2)}) collective-permute-start(f32[8,1,32,128]{3,0,2,1:T(8,128)S(1)} %get-tuple-element.53), channel_id=1, source_target_pairs={{0,1},{1,2},{2,3},{4,5},{5,6},{6,7},{8,9},{9,10},{10,11},{12,13},{... | collective-permute-start | bytes 393224 | tf_op jit(solution)/shard_map/ppermute | solution.py:26
  213.1 7.0 %collective-permute-start.6 = (f32[8,1,32,128]{3,0,2,1:T(8,128)S(1)}, f32[8,1,32,128]{3,0,2,1:T(8,128)S(1)}, u32[]{:S(2)}, u32[]{:S(2)}) collective-permute-start(f32[8,1,32,128]{3,0,2,1:T(8,128)S(1)} %get-tuple-element.46), channel_id=1, source_target_pairs={{1,0},{2,1},{3,2},{5,4},{6,5},{7,6},{9,8},{10,9},{11,10},{13,12},{... | collective-permute-start | bytes 393224 | tf_op jit(solution)/shard_map/ppermute | solution.py:28
  215.0 6.3 %collective-permute-start.7 = (f32[8,1,32,128]{3,0,2,1:T(8,128)S(1)}, f32[8,1,32,128]{3,0,2,1:T(8,128)S(1)}, u32[]{:S(2)}, u32[]{:S(2)}) collective-permute-start(f32[8,1,32,128]{3,0,2,1:T(8,128)S(1)} %get-tuple-element.47), channel_id=1, source_target_pairs={{0,1},{1,2},{2,3},{4,5},{5,6},{6,7},{8,9},{9,10},{10,11},{12,13},{... | collective-permute-start | bytes 393224 | tf_op jit(solution)/shard_map/ppermute | solution.py:26
  222.1 7.0 %collective-permute-start.8 = (f32[8,1,32,128]{3,0,2,1:T(8,128)S(1)}, f32[8,1,32,128]{3,0,2,1:T(8,128)S(1)}, u32[]{:S(2)}, u32[]{:S(2)}) collective-permute-start(f32[8,1,32,128]{3,0,2,1:T(8,128)S(1)} %get-tuple-element.44), channel_id=1, source_target_pairs={{1,0},{2,1},{3,2},{5,4},{6,5},{7,6},{9,8},{10,9},{11,10},{13,12},{... | collective-permute-start | bytes 393224 | tf_op jit(solution)/shard_map/ppermute | solution.py:28
  224.0 6.3 %collective-permute-start.9 = (f32[8,1,32,128]{3,0,2,1:T(8,128)S(1)}, f32[8,1,32,128]{3,0,2,1:T(8,128)S(1)}, u32[]{:S(2)}, u32[]{:S(2)}) collective-permute-start(f32[8,1,32,128]{3,0,2,1:T(8,128)S(1)} %get-tuple-element.45), channel_id=1, source_target_pairs={{0,1},{1,2},{2,3},{4,5},{5,6},{6,7},{8,9},{9,10},{10,11},{12,13},{... | collective-permute-start | bytes 393224 | tf_op jit(solution)/shard_map/ppermute | solution.py:26
